TPU v7x, 32 devices: a whole 2x2x4 slice. The times are simulated.
32 devices in a mesh: row: 8 (over z, x), col: 4 (over y, core).
Axes of the slice: x: 2, y: 2, z: 4, core: 2. Of those that a mesh axis runs over, the one named last changes fastest.
Arguments:
- amplitudes: float32 [4096, 4096], P('row', 'col'), may hold values from -1 to 1, as said below
- interaction: float32 [4096, 4096], P('row', 'col'), may hold values from -9 to 9, as said below
- occ_energy: float32 [4], replicated, may hold values from -2.5 to -0.5
- vir_energy: float32 [1024], replicated, may hold values from 0.2 to 4
Outputs:
- updated: float32 [4096, 4096], P('row', 'col')
- residual: float32 [4096, 4096], P('row', 'col')
Inputs may be any that keep to these rules, and one draw needn't show every extreme that they name: amplitudes is symmetric: it equals its transpose exactly. interaction is symmetric: it equals its transpose exactly.
All inputs are finite; a program needn't handle non-finite values.
Results may differ from a plain program's by a relative error of at most 0.000057.
Values sent between devices are 32-bit elements; how exact they have to be, the bound alone decides.
No kernel may reach another device: no remote copies, remote signals or barrier semaphores. Data moves between devices by JAX's collectives and lax.ppermute only.
A program may use at most 64 MiB of HBM per device.

v0:
```python
import jax
import jax.numpy as jnp
from jax import lax
from jax.sharding import PartitionSpec as P


def swapped(block, axis, distance):
    count = lax.axis_size(axis)
    route = []
    for low in range(count):
        high = low | 1 << distance
        if high != low and high < count:
            route += [(low, high), (high, low)]
    return lax.ppermute(block, axis, route)


def from_behind(block, axis, distance):
    devices = range(lax.axis_size(axis))
    route = [(i - distance, i) for i in devices if i - distance in devices]
    return lax.ppermute(block, axis, route)


def contract(left_tile, right_tile):
    right_panel = lax.all_gather(right_tile, "row", axis=0, tiled=True)
    return jnp.dot(
        lax.all_gather(left_tile, "col", axis=1, tiled=True),
        right_panel,
        precision=lax.Precision.HIGHEST,
        preferred_element_type=jnp.float32,
    )


def diagonal_tile(tile, row_place, col_place):
    tile_rows = tile.shape[0]
    col_count = lax.axis_size("col")
    ratio = lax.axis_size("row") // col_count
    ratio_bits = ratio.bit_length() - 1
    row_bits = lax.axis_size("row").bit_length() - 1
    blocks = tile.reshape(tile_rows, ratio, tile_rows).transpose(1, 2, 0)
    for bit_index in range(row_bits):
        row_flag = row_place // 2**bit_index % 2
        if bit_index < ratio_bits:
            lower = 2**bit_index
            grouped = blocks.reshape(ratio // (2 * lower), 2, lower, tile_rows, tile_rows)
            zero_half = grouped[:, 0]
            one_half = grouped[:, 1]
            outgoing = jnp.where(row_flag == 0, one_half, zero_half)
            incoming = swapped(outgoing, "row", bit_index)
            new_zero = jnp.where(row_flag == 1, incoming, zero_half)
            new_one = jnp.where(row_flag == 0, incoming, one_half)
            blocks = jnp.stack([new_zero, new_one], axis=1).reshape(ratio, tile_rows, tile_rows)
        else:
            col_flag = col_place // 2 ** (bit_index - ratio_bits) % 2
            stride = 2**bit_index * col_count - 2 ** (bit_index - ratio_bits)
            from_above = from_behind(blocks, ("row", "col"), -stride)
            from_below = from_behind(blocks, ("row", "col"), stride)
            incoming = jnp.where(row_flag == 0, from_above, from_below)
            blocks = jnp.where(row_flag != col_flag, incoming, blocks)
    return blocks.transpose(1, 0, 2).reshape(tile_rows, ratio * tile_rows)


def local(amplitudes, interaction, occ_energy, vir_energy):
    tile_rows, tile_cols = amplitudes.shape
    row_place = lax.axis_index("row")
    col_place = lax.axis_index("col")
    product = contract(amplitudes, interaction)
    mirrored = diagonal_tile(product, row_place, col_place)
    gaps = (vir_energy[None, :] - occ_energy[:, None]).reshape(-1)
    row_gap = lax.dynamic_slice_in_dim(gaps, row_place * tile_rows, tile_rows, 0)
    col_gap = lax.dynamic_slice_in_dim(gaps, col_place * tile_cols, tile_cols, 0)
    denom = row_gap[:, None] + col_gap[None, :]
    residual = interaction + product + mirrored + denom * amplitudes
    updated = amplitudes - residual / denom
    return (updated, residual)


def solution(mesh):
    return jax.shard_map(
        local,
        mesh=mesh,
        in_specs=(P("row", "col"), P("row", "col"), P(), P()),
        out_specs=(P("row", "col"), P("row", "col")),
        check_vma=False,
    )
```

profile of v0, /device:TPU:29, one launch (start us, length us, event | category | flops | bytes accessed | tf_op | source)
XLA Modules:
  0.0 543.7 jit_solution(10985203287929512605)
XLA Ops:
  7.2 0.0 all-gather.3.cloned.1.call-start
  7.2 0.7 all-gather.3.cloned.1.call-update
  7.9 0.0 all-gather.5.cloned.1.call-start
  7.9 0.7 all-gather.5.cloned.1.call-update
  8.7 59.6 %all-gather.3.cloned.1.call-done = f32[512,4096]{1,0:T(8,128)} async-done(((f32[512,1024]{1,0:T(8,128)}), f32[512,4096]{1,0:T(8,128)}) %all-gather.3.cloned.1.call-update) | async-done | bytes 8388624 | tf_op jit(solution)/shard_map/all_gather | solution.py:26
  68.3 228.1 %all-gather.5.cloned.1.call-done = f32[4096,1024]{1,0:T(8,128)} async-done(((f32[512,1024]{1,0:T(8,128)}), f32[4096,1024]{1,0:T(8,128)}) %all-gather.5.cloned.1.call-update) | async-done | bytes 16777232 | tf_op jit(solution)/shard_map/all_gather | solution.py:24
  296.4 31.8 %fusion.5 = f32[512,1024]{1,0:T(8,128)} fusion(f32[512,4096]{1,0:T(8,128)} %all-gather.3.cloned.1.call-done, f32[4096,1024]{1,0:T(8,128)} %all-gather.5.cloned.1.call-done), kind=kOutput, calls=%fused_computation.16 | convolution fusion | flops 25769803776 | bytes 27262976 | tf_op jit(solution)/shard_map/dot_general | solution.py:25
  328.1 3.0 reshape.44
  331.2 1.1 broadcast_select_fusion.1
  332.2 0.3 collective-permute-start
  332.6 24.0 %collective-permute-done = f32[1,1,512,512]{2,1,3,0:T(1,128)} collective-permute-done((f32[1,1,512,512]{2,1,3,0:T(1,128)S(1)}, f32[1,1,512,512]{2,1,3,0:T(1,128)}, u32[]{:S(2)}, u32[]{:S(2)}) %collective-permute-start) | collective-permute-done | bytes 1048608 | tf_op jit(solution)/shard_map/ppermute | solution.py:14
  356.6 2.9 fusion.2
  359.5 3.2 maximum_bitcast_fusion
  362.7 4.0 collective-permute-start.1
  366.7 1.3 collective-permute-start.2
  368.0 0.0 copy-start.5
  368.0 0.0 copy-start.6
  368.0 43.3 %collective-permute-done.1 = f32[2,512,512]{1,0,2:T(2,128)S(1)} collective-permute-done((f32[2,512,512]{1,0,2:T(2,128)}, f32[2,512,512]{1,0,2:T(2,128)S(1)}, u32[]{:S(2)}, u32[]{:S(2)}) %collective-permute-start.1) | collective-permute-done | bytes 2097184 | tf_op jit(solution)/shard_map/ppermute | solution.py:20
  411.3 1.3 copy-done.4
  412.7 2.5 collective-permute-done.2
  415.1 4.1 select_select_fusion
  419.2 6.0 %collective-permute-start.3 = (f32[2,512,512]{1,0,2:T(2,128)S(1)}, f32[2,512,512]{1,0,2:T(2,128)}, u32[]{:S(2)}, u32[]{:S(2)}) collective-permute-start(f32[2,512,512]{1,0,2:T(2,128)S(1)} %select_select_fusion), channel_id=1, source_target_pairs={{14,0},{15,1},{16,2},{17,3},{18,4},{19,5},{20,6},{21,7},{22,8},{23... | collective-permute-start | bytes 6291464 | tf_op jit(solution)/shard_map/ppermute | solution.py:20
  425.2 1.3 collective-permute-start.4
  426.6 0.1 subtract_bitcast_fusion
  426.7 0.1 dynamic_slice.6
  426.8 41.9 %collective-permute-done.3 = f32[2,512,512]{1,0,2:T(2,128)} collective-permute-done((f32[2,512,512]{1,0,2:T(2,128)S(1)}, f32[2,512,512]{1,0,2:T(2,128)}, u32[]{:S(2)}, u32[]{:S(2)}) %collective-permute-start.3) | collective-permute-done | bytes 2097184 | tf_op jit(solution)/shard_map/ppermute | solution.py:20
  468.6 52.1 %collective-permute-done.4 = f32[2,512,512]{1,0,2:T(2,128)} collective-permute-done((f32[2,512,512]{1,0,2:T(2,128)S(1)}, f32[2,512,512]{1,0,2:T(2,128)}, u32[]{:S(2)}, u32[]{:S(2)}) %collective-permute-start.4) | collective-permute-done | bytes 2097184 | tf_op jit(solution)/shard_map/ppermute | solution.py:20
  520.7 4.4 select_bitcast_fusion
  525.0 6.2 %copy.6 = f32[512,2,512]{2,1,0:T(2,128)} copy(f32[512,2,512]{0,1,2:T(2,128)} %select_bitcast_fusion) | data formatting | bytes 4194304 | tf_op jit(solution)/shard_map/transpose | solution.py:59
  531.3 2.2 copy.7
  533.5 0.6 copy-done.2
  534.1 2.7 fusion.1
  (12 shorter events, 0.0 us)
Async XLA Ops:
  7.2 61.1 %all-gather.3.cloned.1.call-start = ((), (), s32[]{:S(2)}) async-start(), calls=%async_computation | async-start | bytes 10485760 | tf_op jit(solution)/shard_map/all_gather | solution.py:26
  7.9 288.5 %all-gather.5.cloned.1.call-start = ((), (), s32[]{:S(2)}) async-start(), calls=%async_computation.1 | async-start | bytes 18874368 | tf_op jit(solution)/shard_map/all_gather | solution.py:24
  332.2 24.3 %collective-permute-start = (f32[1,1,512,512]{2,1,3,0:T(1,128)S(1)}, f32[1,1,512,512]{2,1,3,0:T(1,128)}, u32[]{:S(2)}, u32[]{:S(2)}) collective-permute-start(f32[1,1,512,512]{2,1,3,0:T(1,128)S(1)} %broadcast_select_fusion.1), channel_id=1, source_target_pairs={{0,4},{4,0},{8,12},{12,8},{16,20},{20,16},{24,28},{28,24},{1,5},{5... | collective-permute-start | bytes 3145736 | tf_op jit(solution)/shard_map/ppermute | solution.py:14
  359.4 3.2 copy-start
  362.7 48.6 %collective-permute-start.1 = (f32[2,512,512]{1,0,2:T(2,128)}, f32[2,512,512]{1,0,2:T(2,128)S(1)}, u32[]{:S(2)}, u32[]{:S(2)}) collective-permute-start(f32[2,512,512]{1,0,2:T(2,128)} %maximum_bitcast_fusion), channel_id=1, source_target_pairs={{7,0},{8,1},{9,2},{10,3},{11,4},{12,5},{13,6},{14,7},{15,8},{16,9}... | collective-permute-start | bytes 6291464 | tf_op jit(solution)/shard_map/ppermute | solution.py:20
  366.7 48.5 %collective-permute-start.2 = (f32[2,512,512]{1,0,2:T(2,128)}, f32[2,512,512]{1,0,2:T(2,128)}, u32[]{:S(2)}, u32[]{:S(2)}) collective-permute-start(f32[2,512,512]{1,0,2:T(2,128)} %maximum_bitcast_fusion), channel_id=1, source_target_pairs={{0,7},{1,8},{2,9},{3,10},{4,11},{5,12},{6,13},{7,14},{8,15},{9,16}... | collective-permute-start | bytes 6291464 | tf_op jit(solution)/shard_map/ppermute | solution.py:20
  368.0 58.6 %copy-start.5 = (f32[1024]{0:T(1024)S(1)}, f32[1024]{0:T(1024)}, u32[]{:S(2)}) copy-start(f32[1024]{0:T(1024)} %param.7) | copy-start | bytes 12292
  368.0 58.6 %copy-start.6 = (f32[4]{0:T(128)S(1)}, f32[4]{0:T(128)}, u32[]{:S(2)}) copy-start(f32[4]{0:T(128)} %param.6) | copy-start | bytes 52
  411.3 1.3 copy-start.4
  419.2 49.4 %collective-permute-start.3 = (f32[2,512,512]{1,0,2:T(2,128)S(1)}, f32[2,512,512]{1,0,2:T(2,128)}, u32[]{:S(2)}, u32[]{:S(2)}) collective-permute-start(f32[2,512,512]{1,0,2:T(2,128)S(1)} %select_select_fusion), channel_id=1, source_target_pairs={{14,0},{15,1},{16,2},{17,3},{18,4},{19,5},{20,6},{21,7},{22,8},{23... | collective-permute-start | bytes 6291464 | tf_op jit(solution)/shard_map/ppermute | solution.py:20
  425.2 95.4 %collective-permute-start.4 = (f32[2,512,512]{1,0,2:T(2,128)S(1)}, f32[2,512,512]{1,0,2:T(2,128)}, u32[]{:S(2)}, u32[]{:S(2)}) collective-permute-start(f32[2,512,512]{1,0,2:T(2,128)S(1)} %select_select_fusion), channel_id=1, source_target_pairs={{0,14},{1,15},{2,16},{3,17},{4,18},{5,19},{6,20},{7,21},{8,22},{9,... | collective-permute-start | bytes 6291464 | tf_op jit(solution)/shard_map/ppermute | solution.py:20
  525.0 8.5 %copy-start.3 = (f32[512,1024]{1,0:T(8,128)S(1)}, f32[512,1024]{1,0:T(8,128)}, u32[]{:S(2)}) copy-start(f32[512,1024]{1,0:T(8,128)} %fusion.5) | copy-start | bytes 6291460
  531.3 2.2 copy-start.1
  531.3 2.9 copy-start.2
Sparse Core Ops, SparseCore 0:
  9.5 58.6 all-gather.2
  70.4 225.9 all-gather.4
where the time goes:
time: 544 us
  waiting for transfers between devices  453 us (83%)
  matrix products  31.8 us (6%)
  other arithmetic  18.4 us (3%)
  between operations  14.3 us (3%)
  local copies, waits for them, and re-layouts  13.5 us (2%)
  starting transfers between devices  13 us (2%)
    all_gather x1, waiting for transfers between devices, contract(): right_panel = lax.all_gather(right_tile, 'row', axis=0, tiled=True)  228 us
    ppermute x4, waiting for transfers between devices, from_behind(): return lax.ppermute(block, axis, route)  140 us
    all_gather x1, waiting for transfers between devices, contract(): lax.all_gather(left_tile, 'col', axis=1, tiled=True)  59.6 us
    dot_general x1, matrix products, contract(): jnp.dot(lax.all_gather(left_tile, 'col', axis=1, tiled=True), right_panel...  31.8 us
    ppermute x1, waiting for transfers between devices, swapped(): return lax.ppermute(block, axis, route)  24 us
    ppermute x4, starting transfers between devices, from_behind(): return lax.ppermute(block, axis, route)  12.6 us
  transfers between devices with their start and end apart: 7, of which 7 were waited for; matrix products, arithmetic and copies ran while one was open for 0% of the time, Pallas kernels for 0%

commit v1 on v0

--- a/solution.py
+++ b/solution.py
@@ -2,6 +2,22 @@
 import jax.numpy as jnp
 from jax import lax
 from jax.sharding import PartitionSpec as P
+
+
+def gather_around(x, axis, dim):
+    ways, here, lap = (lax.axis_size(axis), lax.axis_index(axis), x.shape[dim])
+    dims = [n * ways if d == dim else n for d, n in enumerate(x.shape)]
+    full = lax.dynamic_update_slice_in_dim(jnp.zeros(dims, x.dtype), x, here * lap, axis=dim)
+    going_up = going_down = x
+    for far in range(1, ways // 2 + 1):
+        going_up = lax.ppermute(going_up, axis, [(d, (d + 1) % ways) for d in range(ways)])
+        full = lax.dynamic_update_slice_in_dim(full, going_up, (here - far) % ways * lap, axis=dim)
+        if 2 * far < ways:
+            going_down = lax.ppermute(going_down, axis, [(d, (d - 1) % ways) for d in range(ways)])
+            full = lax.dynamic_update_slice_in_dim(
+                full, going_down, (here + far) % ways * lap, axis=dim
+            )
+    return full
 
 
 def swapped(block, axis, distance):
@@ -23,7 +39,7 @@
 def contract(left_tile, right_tile):
     right_panel = lax.all_gather(right_tile, "row", axis=0, tiled=True)
     return jnp.dot(
-        lax.all_gather(left_tile, "col", axis=1, tiled=True),
+        gather_around(left_tile, "col", 1),
         right_panel,
         precision=lax.Precision.HIGHEST,
         preferred_element_type=jnp.float32,

time: 544 us -> 484 us (0.89)
  waiting for transfers between devices: 453 us -> 374 us
  local copies, waits for them, and re-layouts: 13.5 us -> 29.6 us
    all_gather x1, waiting for transfers between devices: 228 us -> 154 us  [contract(): right_panel = lax.all_gather(right_tile, 'row', axis=0, tiled=True)]
    all_gather x1 -> x0, waiting for transfers between devices: 59.6 us -> none  [contract(): lax.all_gather(left_tile, 'col', axis=1, tiled=True)]
    ppermute x0 -> x3, waiting for transfers between devices: none -> 54.9 us  [the longest x2 54.9 us: gather_around(): lax.ppermute(going_up, axis, [(d, (d + 1) % ways) for d in range(ways)])]
    dynamic_update_slice x0 -> x4, local copies, waits for them, and re-layouts: none -> 10.9 us  [the longest x2 6.27 us: gather_around(): lax.dynamic_update_slice_in_dim(full, going_up, (here - far) % ways * lap...]
  transfers between devices with their start and end apart: 7 -> 9, of which waited for: 7 -> 8; matrix products, arithmetic and copies ran while one was open for 0% -> 3% of each run, Pallas kernels for 0% -> 0%
where the time goes in v1:
time: 484 us
  waiting for transfers between devices  374 us (77%)
  matrix products  31.8 us (7%)
  local copies, waits for them, and re-layouts  29.6 us (6%)
  other arithmetic  18.4 us (4%)
  starting transfers between devices  16.1 us (3%)
  between operations  14.3 us (3%)
    all_gather x1, waiting for transfers between devices, contract(): right_panel = lax.all_gather(right_tile, 'row', axis=0, tiled=True)  154 us
    ppermute x4, waiting for transfers between devices, from_behind(): return lax.ppermute(block, axis, route)  140 us
    ppermute x2, waiting for transfers between devices, gather_around(): lax.ppermute(going_up, axis, [(d, (d + 1) % ways) for d in range(ways)])  54.9 us
    dot_general x1, matrix products, contract(): jnp.dot(gather_around(left_tile, 'col', 1), right_panel, precision=lax.Pr...  31.8 us
    ppermute x1, waiting for transfers between devices, swapped(): return lax.ppermute(block, axis, route)  24 us
    ppermute x4, starting transfers between devices, from_behind(): return lax.ppermute(block, axis, route)  12.4 us
  transfers between devices with their start and end apart: 9, of which 8 were waited for; matrix products, arithmetic and copies ran while one was open for 3% of the time, Pallas kernels for 0%

profile of v1, /device:TPU:29, one launch (start us, length us, event | category | flops | bytes accessed | tf_op | source)
XLA Modules:
  0.0 483.7 jit_solution(2778988563064463935)
XLA Ops:
  7.2 0.7 all-gather.2.cloned.1.call-update
  7.9 0.8 copy-done.1
  8.8 0.8 collective-permute-start
  9.5 43.6 %collective-permute-done = f32[512,1024]{1,0:T(8,128)} collective-permute-done((f32[512,1024]{1,0:T(8,128)S(1)}, f32[512,1024]{1,0:T(8,128)}, u32[]{:S(2)}, u32[]{:S(2)}) %collective-permute-start) | collective-permute-done | bytes 2097184 | tf_op jit(solution)/shard_map/ppermute | solution.py:13
  53.2 2.6 collective-permute-start.2
  55.8 4.3 broadcast_in_dim.2
  60.0 1.4 constant_dynamic-update-slice_fusion.3
  61.5 3.1 constant_dynamic-update-slice_fusion.2
  64.6 3.2 constant_dynamic-update-slice_fusion.1
  67.8 11.3 %collective-permute-done.2 = f32[512,1024]{1,0:T(8,128)} collective-permute-done((f32[512,1024]{1,0:T(8,128)}, f32[512,1024]{1,0:T(8,128)}, u32[]{:S(2)}, u32[]{:S(2)}) %collective-permute-start.2) | collective-permute-done | bytes 2097184 | tf_op jit(solution)/shard_map/ppermute | solution.py:13
  79.1 3.1 constant_dynamic-update-slice_fusion
  82.2 154.3 %all-gather.2.cloned.1.call-done = f32[4096,1024]{1,0:T(8,128)} async-done(((f32[512,1024]{1,0:T(8,128)}), f32[4096,1024]{1,0:T(8,128)}) %all-gather.2.cloned.1.call-update) | async-done | bytes 16777232 | tf_op jit(solution)/shard_map/all_gather | solution.py:40
  236.5 31.8 %fusion.5 = f32[512,1024]{1,0:T(8,128)} fusion(f32[512,4096]{1,0:T(8,128)} %constant_dynamic-update-slice_fusion, f32[4096,1024]{1,0:T(8,128)} %all-gather.2.cloned.1.call-done), kind=kOutput, calls=%fused_computation.20 | convolution fusion | flops 25769803776 | bytes 27262976 | tf_op jit(solution)/shard_map/dot_general | solution.py:41
  268.3 3.0 reshape.44
  271.3 1.1 broadcast_select_fusion.1
  272.7 24.0 %collective-permute-done.3 = f32[1,1,512,512]{2,1,3,0:T(1,128)} collective-permute-done((f32[1,1,512,512]{2,1,3,0:T(1,128)S(1)}, f32[1,1,512,512]{2,1,3,0:T(1,128)}, u32[]{:S(2)}, u32[]{:S(2)}) %collective-permute-start.3) | collective-permute-done | bytes 1048608 | tf_op jit(solution)/shard_map/ppermute | solution.py:30
  296.7 2.9 fusion.2
  299.6 3.2 maximum_bitcast_fusion
  302.8 3.8 collective-permute-start.4
  306.6 1.3 collective-permute-start.5
  308.0 43.5 %collective-permute-done.4 = f32[2,512,512]{1,0,2:T(2,128)S(1)} collective-permute-done((f32[2,512,512]{1,0,2:T(2,128)}, f32[2,512,512]{1,0,2:T(2,128)S(1)}, u32[]{:S(2)}, u32[]{:S(2)}) %collective-permute-start.4) | collective-permute-done | bytes 2097184 | tf_op jit(solution)/shard_map/ppermute | solution.py:36
  351.5 1.3 copy-done.5
  352.8 2.3 collective-permute-done.5
  355.1 4.1 select_select_fusion
  359.2 6.0 %collective-permute-start.6 = (f32[2,512,512]{1,0,2:T(2,128)S(1)}, f32[2,512,512]{1,0,2:T(2,128)}, u32[]{:S(2)}, u32[]{:S(2)}) collective-permute-start(f32[2,512,512]{1,0,2:T(2,128)S(1)} %select_select_fusion), channel_id=1, source_target_pairs={{14,0},{15,1},{16,2},{17,3},{18,4},{19,5},{20,6},{21,7},{22,8},{23... | collective-permute-start | bytes 6291464 | tf_op jit(solution)/shard_map/ppermute | solution.py:36
  365.2 1.3 collective-permute-start.7
  366.7 41.8 %collective-permute-done.6 = f32[2,512,512]{1,0,2:T(2,128)} collective-permute-done((f32[2,512,512]{1,0,2:T(2,128)S(1)}, f32[2,512,512]{1,0,2:T(2,128)}, u32[]{:S(2)}, u32[]{:S(2)}) %collective-permute-start.6) | collective-permute-done | bytes 2097184 | tf_op jit(solution)/shard_map/ppermute | solution.py:36
  408.6 52.1 %collective-permute-done.7 = f32[2,512,512]{1,0,2:T(2,128)} collective-permute-done((f32[2,512,512]{1,0,2:T(2,128)S(1)}, f32[2,512,512]{1,0,2:T(2,128)}, u32[]{:S(2)}, u32[]{:S(2)}) %collective-permute-start.7) | collective-permute-done | bytes 2097184 | tf_op jit(solution)/shard_map/ppermute | solution.py:36
  460.7 4.4 select_bitcast_fusion
  465.0 6.2 %copy.6 = f32[512,2,512]{2,1,0:T(2,128)} copy(f32[512,2,512]{0,1,2:T(2,128)} %select_bitcast_fusion) | data formatting | bytes 4194304 | tf_op jit(solution)/shard_map/transpose | solution.py:75
  471.3 2.2 copy.7
  474.1 2.7 fusion.1
  (22 shorter events, 1.2 us)
Async XLA Ops:
  7.2 1.6 copy-start.1
  7.2 229.3 %all-gather.2.cloned.1.call-start = ((), (), s32[]{:S(2)}) async-start(), calls=%async_computation | async-start | bytes 18874368 | tf_op jit(solution)/shard_map/all_gather | solution.py:40
  8.8 44.4 %collective-permute-start = (f32[512,1024]{1,0:T(8,128)S(1)}, f32[512,1024]{1,0:T(8,128)}, u32[]{:S(2)}, u32[]{:S(2)}) collective-permute-start(f32[512,1024]{1,0:T(8,128)S(1)} %copy-done.1), channel_id=1, source_target_pairs={{0,1},{1,2},{2,3},{3,0},{4,5},{5,6},{6,7},{7,4},{8,9},{9,10},{10,1... | collective-permute-start | bytes 6291464 | tf_op jit(solution)/shard_map/ppermute | solution.py:13
  9.5 55.1 %collective-permute-start.1 = (f32[512,1024]{1,0:T(8,128)S(1)}, f32[512,1024]{1,0:T(8,128)}, u32[]{:S(2)}, u32[]{:S(2)}) collective-permute-start(f32[512,1024]{1,0:T(8,128)S(1)} %copy-done.1), channel_id=1, source_target_pairs={{0,3},{1,0},{2,1},{3,2},{4,7},{5,4},{6,5},{7,6},{8,11},{9,8},{10,9... | collective-permute-start | bytes 6291464 | tf_op jit(solution)/shard_map/ppermute | solution.py:16
  53.2 25.9 %collective-permute-start.2 = (f32[512,1024]{1,0:T(8,128)}, f32[512,1024]{1,0:T(8,128)}, u32[]{:S(2)}, u32[]{:S(2)}) collective-permute-start(f32[512,1024]{1,0:T(8,128)} %collective-permute-done), channel_id=1, source_target_pairs={{0,1},{1,2},{2,3},{3,0},{4,5},{5,6},{6,7},{7,4},{8,9},{9,10},{10,1... | collective-permute-start | bytes 6291464 | tf_op jit(solution)/shard_map/ppermute | solution.py:13
  272.4 24.3 %collective-permute-start.3 = (f32[1,1,512,512]{2,1,3,0:T(1,128)S(1)}, f32[1,1,512,512]{2,1,3,0:T(1,128)}, u32[]{:S(2)}, u32[]{:S(2)}) collective-permute-start(f32[1,1,512,512]{2,1,3,0:T(1,128)S(1)} %broadcast_select_fusion.1), channel_id=1, source_target_pairs={{0,4},{4,0},{8,12},{12,8},{16,20},{20,16},{24,28},{28,24},{1,5},{5... | collective-permute-start | bytes 3145736 | tf_op jit(solution)/shard_map/ppermute | solution.py:30
  299.6 3.2 copy-start
  302.8 48.6 %collective-permute-start.4 = (f32[2,512,512]{1,0,2:T(2,128)}, f32[2,512,512]{1,0,2:T(2,128)S(1)}, u32[]{:S(2)}, u32[]{:S(2)}) collective-permute-start(f32[2,512,512]{1,0,2:T(2,128)} %maximum_bitcast_fusion), channel_id=1, source_target_pairs={{7,0},{8,1},{9,2},{10,3},{11,4},{12,5},{13,6},{14,7},{15,8},{16,9}... | collective-permute-start | bytes 6291464 | tf_op jit(solution)/shard_map/ppermute | solution.py:36
  306.6 48.5 %collective-permute-start.5 = (f32[2,512,512]{1,0,2:T(2,128)}, f32[2,512,512]{1,0,2:T(2,128)}, u32[]{:S(2)}, u32[]{:S(2)}) collective-permute-start(f32[2,512,512]{1,0,2:T(2,128)} %maximum_bitcast_fusion), channel_id=1, source_target_pairs={{0,7},{1,8},{2,9},{3,10},{4,11},{5,12},{6,13},{7,14},{8,15},{9,16}... | collective-permute-start | bytes 6291464 | tf_op jit(solution)/shard_map/ppermute | solution.py:36
  308.0 58.6 %copy-start.6 = (f32[1024]{0:T(1024)S(1)}, f32[1024]{0:T(1024)}, u32[]{:S(2)}) copy-start(f32[1024]{0:T(1024)} %param.7) | copy-start | bytes 12292
  308.0 58.6 %copy-start.7 = (f32[4]{0:T(128)S(1)}, f32[4]{0:T(128)}, u32[]{:S(2)}) copy-start(f32[4]{0:T(128)} %param.6) | copy-start | bytes 52
  351.5 1.3 copy-start.5
  359.2 49.4 %collective-permute-start.6 = (f32[2,512,512]{1,0,2:T(2,128)S(1)}, f32[2,512,512]{1,0,2:T(2,128)}, u32[]{:S(2)}, u32[]{:S(2)}) collective-permute-start(f32[2,512,512]{1,0,2:T(2,128)S(1)} %select_select_fusion), channel_id=1, source_target_pairs={{14,0},{15,1},{16,2},{17,3},{18,4},{19,5},{20,6},{21,7},{22,8},{23... | collective-permute-start | bytes 6291464 | tf_op jit(solution)/shard_map/ppermute | solution.py:36
  365.2 95.4 %collective-permute-start.7 = (f32[2,512,512]{1,0,2:T(2,128)S(1)}, f32[2,512,512]{1,0,2:T(2,128)}, u32[]{:S(2)}, u32[]{:S(2)}) collective-permute-start(f32[2,512,512]{1,0,2:T(2,128)S(1)} %select_select_fusion), channel_id=1, source_target_pairs={{0,14},{1,15},{2,16},{3,17},{4,18},{5,19},{6,20},{7,21},{8,22},{9,... | collective-permute-start | bytes 6291464 | tf_op jit(solution)/shard_map/ppermute | solution.py:36
  465.0 8.5 %copy-start.4 = (f32[512,1024]{1,0:T(8,128)S(1)}, f32[512,1024]{1,0:T(8,128)}, u32[]{:S(2)}) copy-start(f32[512,1024]{1,0:T(8,128)} %fusion.5) | copy-start | bytes 6291460
  471.3 2.2 copy-start.2
  471.3 2.9 copy-start.3
Sparse Core Ops, SparseCore 0:
  10.1 226.3 all-gather.1
